TPU v7x, 256 devices: a whole 4x4x8 slice. The times are simulated.
256 devices in a mesh: sub: 32 (over z_hi, y, core), grp: 8 (over z_lo, x).
Axes of the slice: x: 4, y: 4, z: 8 (z_hi: 4, z_lo: 2; z = z_hi * 2 + z_lo), core: 2. Of those that a mesh axis runs over, the one named last changes fastest.
Arguments:
- right_side: float32 [8, 32, 1024, 128], P('grp', 'sub'), may hold values from -13 to 13
- schur_blocks: bfloat16 [8, 32, 2048, 2048], P('grp', 'sub'), may hold values from -2 to 7, as said below
- occupancy: int32 [8, 32, 1024], P('grp', 'sub'), may hold values 0 or 1
- precond_weights: float32 [8, 32, 1024], P('grp', 'sub'), may hold values from 0.1 to 1
- coarse_basis: float32 [8, 32, 8, 1024], P('grp', 'sub'), may hold values from -0.1875 to 0.1875
- coarse_inverse: float32 [8, 256, 256], P('grp', 'sub'), may hold values from -1 to 5, as said below
Outputs:
- solution: float32 [8, 32, 1024, 128], P('grp', 'sub')
- residual: float32 [8, 32, 1024, 128], P('grp', 'sub')
Inputs may be any that keep to these rules, and one draw needn't show every extreme that they name: `schur_blocks`: each strip's block is symmetric positive definite, diagonal entries between 1.4 and 6.1. `coarse_inverse`: each group's matrix is symmetric positive definite, diagonal entries between 0.9 and 4.2.
All inputs are finite; a program needn't handle non-finite values. No bound on the sum of `occupancy` on one device may be relied on, other than what follows from the above.
Results may differ from a plain program's by a relative error of at most 0.035.
Values may be sent and summed in bfloat16 or wider, within the bound.
A program may use at most 64 MiB of HBM per device.

v0:
```python
import jax
import jax.numpy as jnp
from jax import lax
from jax.sharding import PartitionSpec as P

ITERS = 3


def passed_along(block, axis, distance):
    devices = range(lax.axis_size(axis))
    route = [((i - distance) % len(devices), i) for i in devices]
    return lax.ppermute(block, axis, route)


def shifted(value, axis, steps):
    count = lax.axis_size(axis)
    initial, last = (max(0, -steps), min(count, count - steps))
    return lax.ppermute(value, axis, [(source, source + steps) for source in range(initial, last)])


def local(right_side, schur_blocks, occupancy, precond_weights, coarse_basis, coarse_inverse):
    schur_block = schur_blocks[0, 0]
    free_cells = occupancy[0, 0].astype(jnp.float32)[:, None]
    weight_col = precond_weights[0, 0][:, None]
    basis_rows = coarse_basis[0, 0]
    inverse_rows = coarse_inverse[0]
    source = right_side[0, 0]
    face_cells = source.shape[0]
    group_count = lax.axis_size("sub")
    position = lax.axis_index("sub")
    contract = (((0,), (0,)), ((), ()))

    def precondition(residual):
        coarse = jnp.dot(basis_rows, residual, precision=lax.Precision.HIGHEST)
        group_coarse = lax.all_gather(coarse, "sub", axis=0, tiled=True)
        solved = jnp.dot(inverse_rows, group_coarse, precision=lax.Precision.HIGHEST)
        spread_back = lax.dot_general(basis_rows, solved, contract, precision=lax.Precision.HIGHEST)
        return weight_col * residual + spread_back

    def precond_inner(residual, precond):
        return lax.psum(jnp.sum(residual * precond, axis=0), ("sub", "grp"))

    solution = jnp.zeros_like(source)
    residual = source
    precond = precondition(residual)
    direction = precond
    inner_now = precond_inner(residual, precond)
    for iteration in range(ITERS):
        masked = (free_cells * direction).astype(jnp.bfloat16)
        beside_all = passed_along(masked, "sub", -1)
        crossed = shifted(beside_all, "grp", -1)
        following = jnp.where(position == group_count - 1, crossed, beside_all)
        stacked = jnp.concatenate([masked, following], axis=0)
        product = jnp.dot(schur_block, stacked, preferred_element_type=jnp.float32)
        outgoing = product[face_cells:].astype(jnp.bfloat16)
        behind = passed_along(outgoing, "sub", 1)
        crossed_back = shifted(behind, "grp", 1)
        incoming = jnp.where(position == 0, crossed_back, behind)
        image = (
            free_cells * (product[:face_cells] + incoming.astype(jnp.float32))
            + (1.0 - free_cells) * direction
        )
        step_size = inner_now / lax.psum(jnp.sum(direction * image, axis=0), ("sub", "grp"))
        solution = solution + step_size * direction
        residual = residual - step_size * image
        if iteration + 1 < ITERS:
            precond = precondition(residual)
            inner_next = precond_inner(residual, precond)
            direction = precond + inner_next / inner_now * direction
            inner_now = inner_next
    return (solution[None, None], residual[None, None])


def solution(mesh):
    return jax.shard_map(
        local,
        mesh=mesh,
        in_specs=(
            P("grp", "sub", None, None),
            P("grp", "sub", None, None),
            P("grp", "sub", None),
            P("grp", "sub", None),
            P("grp", "sub", None, None),
            P("grp", "sub", None),
        ),
        out_specs=(P("grp", "sub", None, None), P("grp", "sub", None, None)),
        check_vma=False,
    )
```

profile of v0, /device:TPU:2, one launch (start us, length us, event | category | flops | bytes accessed | tf_op | source)
XLA Modules:
  0.0 647.6 jit_solution(17180566580435164239)
XLA Ops:
  0.6 0.7 convert_element_type.34
  1.3 1.2 copy.11
  2.6 1.4 fusion.33
  4.0 47.9 %all_gather.9 = f32[256,128]{1,0:T(8,128)S(1)} all-gather(f32[8,128]{1,0:T(8,128)S(1)} %fusion.33), channel_id=1, replica_groups=mesh['sub'=32,'grp'=8] {'sub'}, dimensions={0}, use_global_device_ids=true | all-gather | bytes 135168 | tf_op jit(solution)/shard_map/all_gather | solution.py:35
  51.9 1.1 fusion.46
  53.0 1.3 multiply_convert_fusion.2
  54.4 6.7 %collective-permute-done = bf16[1024,128]{0,1:T(8,128)(2,1)S(1)} collective-permute-done((bf16[1024,128]{0,1:T(8,128)(2,1)S(1)}, bf16[1024,128]{0,1:T(8,128)(2,1)S(1)}, u32[]{:S(2)}, u32[]{:S(2)}) %collective-permute-start) | collective-permute-done | bytes 262176 | tf_op jit(solution)/shard_map/ppermute | solution.py:12
  61.0 2.4 collective-permute-start.1
  63.5 7.1 %collective-permute-done.1 = bf16[1024,128]{0,1:T(8,128)(2,1)S(1)} collective-permute-done((bf16[1024,128]{0,1:T(8,128)(2,1)S(1)}, bf16[1024,128]{0,1:T(8,128)(2,1)S(1)}, u32[]{:S(2)}, u32[]{:S(2)}) %collective-permute-start.1) | collective-permute-done | bytes 262176 | tf_op jit(solution)/shard_map/ppermute | solution.py:18
  70.6 6.3 fusion.6
  77.0 10.0 %collective-permute-done.2 = bf16[1024,128]{0,1:T(8,128)(2,1)S(1)} collective-permute-done((bf16[1024,128]{0,1:T(8,128)(2,1)S(1)}, bf16[1024,128]{0,1:T(8,128)(2,1)S(1)}, u32[]{:S(2)}, u32[]{:S(2)}) %collective-permute-start.2) | collective-permute-done | bytes 262176 | tf_op jit(solution)/shard_map/ppermute | solution.py:12
  87.0 3.4 collective-permute-start.3
  90.4 4.8 collective-permute-done.3
  95.3 0.3 multiply_reduce_fusion.4
  95.5 76.7 %all-reduce = (f32[128]{0:T(128)S(1)}, f32[128]{0:T(128)S(1)}) all-reduce(f32[128]{0:T(128)S(1)} %get-tuple-element.7, f32[128]{0:T(128)S(1)} %get-tuple-element.6), channel_id=1, replica_groups=mesh['sub'=32,'grp'=8] {'sub','grp'}, use_global_device_ids=true, to_apply=%region_1.0 | all-reduce | flops 256 | bytes 2048 | tf_op jit(solution)/shard_map/psum | solution.py:41
  172.4 0.5 convolution_bitcast_fusion.4
  172.9 40.4 %all_gather.10 = f32[256,128]{1,0:T(8,128)S(1)} all-gather(f32[8,128]{1,0:T(8,128)S(1)} %convolution_bitcast_fusion.4), channel_id=1, replica_groups=mesh['sub'=32,'grp'=8] {'sub'}, dimensions={0}, use_global_device_ids=true | all-gather | bytes 135168 | tf_op jit(solution)/shard_map/all_gather | solution.py:35
  213.4 0.4 fusion.44
  213.8 0.7 multiply_reduce_fusion.3
  214.4 73.8 %psum.44 = f32[128]{0:T(128)S(1)} all-reduce(f32[128]{0:T(128)S(1)} %get-tuple-element.18), channel_id=1, replica_groups=mesh['sub'=32,'grp'=8] {'sub','grp'}, use_global_device_ids=true, to_apply=%region_5.6 | all-reduce | flops 128 | bytes 1024 | tf_op jit(solution)/shard_map/psum | solution.py:41
  288.4 1.4 collective-permute-start.4
  289.8 4.0 collective-permute-done.4
  293.8 4.2 collective-permute-start.5
  298.0 6.2 collective-permute-done.5
  304.3 6.3 fusion.9
  310.8 12.8 %collective-permute-done.6 = bf16[1024,128]{0,1:T(8,128)(2,1)S(1)} collective-permute-done((bf16[1024,128]{0,1:T(8,128)(2,1)S(1)}, bf16[1024,128]{0,1:T(8,128)(2,1)S(1)}, u32[]{:S(2)}, u32[]{:S(2)}) %collective-permute-start.6) | collective-permute-done | bytes 262176 | tf_op jit(solution)/shard_map/ppermute | solution.py:12
  323.6 2.8 collective-permute-start.7
  326.4 5.5 collective-permute-done.7
  332.1 73.9 %psum.45 = f32[128]{0:T(128)S(1)} all-reduce(f32[128]{0:T(128)S(1)} %multiply_reduce_fusion.2), channel_id=1, replica_groups=mesh['sub'=32,'grp'=8] {'sub','grp'}, use_global_device_ids=true, to_apply=%region_7.8 | all-reduce | flops 128 | bytes 1024 | tf_op jit(solution)/shard_map/psum | solution.py:63
  406.1 1.1 multiply_subtract_fusion
  407.2 0.5 convolution_bitcast_fusion.3
  407.7 39.3 %all_gather.11 = f32[256,128]{1,0:T(8,128)S(1)} all-gather(f32[8,128]{1,0:T(8,128)S(1)} %convolution_bitcast_fusion.3), channel_id=1, replica_groups=mesh['sub'=32,'grp'=8] {'sub'}, dimensions={0}, use_global_device_ids=true | all-gather | bytes 135168 | tf_op jit(solution)/shard_map/all_gather | solution.py:35
  447.0 0.4 fusion.42
  447.4 0.7 multiply_reduce_fusion.1
  448.1 73.8 %psum.46 = f32[128]{0:T(128)S(1)} all-reduce(f32[128]{0:T(128)S(1)} %get-tuple-element.20), channel_id=1, replica_groups=mesh['sub'=32,'grp'=8] {'sub','grp'}, use_global_device_ids=true, to_apply=%region_9.10 | all-reduce | flops 128 | bytes 1024 | tf_op jit(solution)/shard_map/psum | solution.py:41
  522.1 2.5 collective-permute-start.8
  524.6 4.0 collective-permute-done.8
  528.6 2.8 collective-permute-start.9
  531.4 6.5 collective-permute-done.9
  537.9 6.3 fusion.12
  544.3 12.8 %collective-permute-done.10 = bf16[1024,128]{0,1:T(8,128)(2,1)S(1)} collective-permute-done((bf16[1024,128]{0,1:T(8,128)(2,1)S(1)}, bf16[1024,128]{0,1:T(8,128)(2,1)S(1)}, u32[]{:S(2)}, u32[]{:S(2)}) %collective-permute-start.10) | collective-permute-done | bytes 262176 | tf_op jit(solution)/shard_map/ppermute | solution.py:12
  557.1 1.9 collective-permute-start.11
  559.1 6.3 collective-permute-done.11
  565.4 0.7 copy-done.2
  566.3 75.0 %psum.47 = f32[128]{0:T(128)S(1)} all-reduce(f32[128]{0:T(128)S(1)} %multiply_reduce_fusion), channel_id=1, replica_groups=mesh['sub'=32,'grp'=8] {'sub','grp'}, use_global_device_ids=true, to_apply=%region_11.12 | all-reduce | flops 128 | bytes 1024 | tf_op jit(solution)/shard_map/psum | solution.py:63
  641.4 2.2 subtract_bitcast_fusion
  643.6 2.0 copy.13
  645.6 2.0 copy.12
  (30 shorter events, 1.7 us)
Async XLA Ops:
  0.6 2.0 copy-start
  54.2 159.1 %copy-start.3 = (f32[1,8,256]{2,1,0:T(8,128)S(1)}, f32[1,8,256]{2,1,0:T(8,128)}, u32[]{:S(2)}) copy-start(f32[1,8,256]{2,1,0:T(8,128)} %param.11) | copy-start | bytes 24580
  54.3 6.8 %collective-permute-start = (bf16[1024,128]{0,1:T(8,128)(2,1)S(1)}, bf16[1024,128]{0,1:T(8,128)(2,1)S(1)}, u32[]{:S(2)}, u32[]{:S(2)}) collective-permute-start(bf16[1024,128]{0,1:T(8,128)(2,1)S(1)} %get-tuple-element.16), channel_id=1, source_target_pairs={{8,0},{16,8},{24,16},{32,24},{40,32},{48,40},{56,48},{64,56},{72,6... | collective-permute-start | bytes 786440 | tf_op jit(solution)/shard_map/ppermute | solution.py:12
  61.0 9.5 %collective-permute-start.1 = (bf16[1024,128]{0,1:T(8,128)(2,1)S(1)}, bf16[1024,128]{0,1:T(8,128)(2,1)S(1)}, u32[]{:S(2)}, u32[]{:S(2)}) collective-permute-start(bf16[1024,128]{0,1:T(8,128)(2,1)S(1)} %collective-permute-done), channel_id=1, source_target_pairs={{1,0},{2,1},{3,2},{4,3},{5,4},{6,5},{7,6},{9,8},{10,9},{11,10},{12... | collective-permute-start | bytes 786440 | tf_op jit(solution)/shard_map/ppermute | solution.py:18
  63.5 150.3 %copy-start.4 = (f32[1,1,1024]{2,1,0:T(1,128)S(1)}, f32[1,1,1024]{2,1,0:T(1,128)}, u32[]{:S(2)}) copy-start(f32[1,1,1024]{2,1,0:T(1,128)} %param.9) | copy-start | bytes 12292
  76.9 10.1 %collective-permute-start.2 = (bf16[1024,128]{0,1:T(8,128)(2,1)S(1)}, bf16[1024,128]{0,1:T(8,128)(2,1)S(1)}, u32[]{:S(2)}, u32[]{:S(2)}) collective-permute-start(bf16[1024,128]{0,1:T(8,128)(2,1)S(1)} %slice.65), channel_id=1, source_target_pairs={{248,0},{0,8},{8,16},{16,24},{24,32},{32,40},{40,48},{48,56},{56,6... | collective-permute-start | bytes 786440 | tf_op jit(solution)/shard_map/ppermute | solution.py:12
  87.0 8.3 %collective-permute-start.3 = (bf16[1024,128]{0,1:T(8,128)(2,1)S(1)}, bf16[1024,128]{0,1:T(8,128)(2,1)S(1)}, u32[]{:S(2)}, u32[]{:S(2)}) collective-permute-start(bf16[1024,128]{0,1:T(8,128)(2,1)S(1)} %collective-permute-done.2), channel_id=1, source_target_pairs={{0,1},{1,2},{2,3},{3,4},{4,5},{5,6},{6,7},{8,9},{9,10},{10,11},{11... | collective-permute-start | bytes 786440 | tf_op jit(solution)/shard_map/ppermute | solution.py:18
  288.4 5.4 collective-permute-start.4
  293.8 10.4 %collective-permute-start.5 = (bf16[1024,128]{0,1:T(8,128)(2,1)S(1)}, bf16[1024,128]{0,1:T(8,128)(2,1)S(1)}, u32[]{:S(2)}, u32[]{:S(2)}) collective-permute-start(bf16[1024,128]{0,1:T(8,128)(2,1)S(1)} %collective-permute-done.4), channel_id=1, source_target_pairs={{1,0},{2,1},{3,2},{4,3},{5,4},{6,5},{7,6},{9,8},{10,9},{11,10},{12... | collective-permute-start | bytes 786440 | tf_op jit(solution)/shard_map/ppermute | solution.py:18
  310.6 13.1 %collective-permute-start.6 = (bf16[1024,128]{0,1:T(8,128)(2,1)S(1)}, bf16[1024,128]{0,1:T(8,128)(2,1)S(1)}, u32[]{:S(2)}, u32[]{:S(2)}) collective-permute-start(bf16[1024,128]{0,1:T(8,128)(2,1)S(1)} %slice.64), channel_id=1, source_target_pairs={{248,0},{0,8},{8,16},{16,24},{24,32},{32,40},{40,48},{48,56},{56,6... | collective-permute-start | bytes 786440 | tf_op jit(solution)/shard_map/ppermute | solution.py:12
  323.6 8.3 %collective-permute-start.7 = (bf16[1024,128]{0,1:T(8,128)(2,1)S(1)}, bf16[1024,128]{0,1:T(8,128)(2,1)S(1)}, u32[]{:S(2)}, u32[]{:S(2)}) collective-permute-start(bf16[1024,128]{0,1:T(8,128)(2,1)S(1)} %collective-permute-done.6), channel_id=1, source_target_pairs={{0,1},{1,2},{2,3},{3,4},{4,5},{5,6},{6,7},{8,9},{9,10},{10,11},{11... | collective-permute-start | bytes 786440 | tf_op jit(solution)/shard_map/ppermute | solution.py:18
  331.9 74.2 %copy-start.1 = (bf16[1024,128]{0,1:T(8,128)(2,1)}, bf16[1024,128]{0,1:T(8,128)(2,1)S(1)}, u32[]{:S(2)}) copy-start(bf16[1024,128]{0,1:T(8,128)(2,1)S(1)} %collective-permute-done.7) | copy-start | bytes 786436
  522.1 6.5 %collective-permute-start.8 = (bf16[1024,128]{0,1:T(8,128)(2,1)S(1)}, bf16[1024,128]{0,1:T(8,128)(2,1)S(1)}, u32[]{:S(2)}, u32[]{:S(2)}) collective-permute-start(bf16[1024,128]{0,1:T(8,128)(2,1)S(1)} %get-tuple-element.10), channel_id=1, source_target_pairs={{8,0},{16,8},{24,16},{32,24},{40,32},{48,40},{56,48},{64,56},{72,6... | collective-permute-start | bytes 786440 | tf_op jit(solution)/shard_map/ppermute | solution.py:12
  528.6 9.3 %collective-permute-start.9 = (bf16[1024,128]{0,1:T(8,128)(2,1)S(1)}, bf16[1024,128]{0,1:T(8,128)(2,1)S(1)}, u32[]{:S(2)}, u32[]{:S(2)}) collective-permute-start(bf16[1024,128]{0,1:T(8,128)(2,1)S(1)} %collective-permute-done.8), channel_id=1, source_target_pairs={{1,0},{2,1},{3,2},{4,3},{5,4},{6,5},{7,6},{9,8},{10,9},{11,10},{12... | collective-permute-start | bytes 786440 | tf_op jit(solution)/shard_map/ppermute | solution.py:18
  544.2 12.9 %collective-permute-start.10 = (bf16[1024,128]{0,1:T(8,128)(2,1)S(1)}, bf16[1024,128]{0,1:T(8,128)(2,1)S(1)}, u32[]{:S(2)}, u32[]{:S(2)}) collective-permute-start(bf16[1024,128]{0,1:T(8,128)(2,1)S(1)} %slice.63), channel_id=1, source_target_pairs={{248,0},{0,8},{8,16},{16,24},{24,32},{32,40},{40,48},{48,56},{56,6... | collective-permute-start | bytes 786440 | tf_op jit(solution)/shard_map/ppermute | solution.py:12
  557.1 8.3 %collective-permute-start.11 = (bf16[1024,128]{0,1:T(8,128)(2,1)S(1)}, bf16[1024,128]{0,1:T(8,128)(2,1)S(1)}, u32[]{:S(2)}, u32[]{:S(2)}) collective-permute-start(bf16[1024,128]{0,1:T(8,128)(2,1)S(1)} %collective-permute-done.10), channel_id=1, source_target_pairs={{0,1},{1,2},{2,3},{3,4},{4,5},{5,6},{6,7},{8,9},{9,10},{10,11},{11... | collective-permute-start | bytes 786440 | tf_op jit(solution)/shard_map/ppermute | solution.py:18
  565.4 0.7 copy-start.2
where the time goes:
time: 649 us; the launch traced here: 648 us
  blocking collectives  501 us (77%)
  waiting for transfers between devices  86.7 us (13%)
  matrix products  25.7 us (4%)
  starting transfers between devices  21.9 us (3%)
    psum x3, blocking collectives, precond_inner(): return lax.psum(jnp.sum(residual * precond, axis=0), ('sub', 'grp'))  224 us
    psum x2, blocking collectives, local(): lax.psum(jnp.sum(direction * image, axis=0), ('sub', 'grp'))  149 us
    all_gather x3, blocking collectives, precondition(): group_coarse = lax.all_gather(coarse, 'sub', axis=0, tiled=True)  128 us
    ppermute x6, waiting for transfers between devices, passed_along(): return lax.ppermute(block, axis, route)  50.4 us
    ppermute x6, waiting for transfers between devices, shifted(): lax.ppermute(value, axis, [(source, source + steps) for source in range(i...  36.4 us
    dot_general x3, matrix products, local(): product = jnp.dot(schur_block, stacked, preferred_element_type=jnp.float32)  18.8 us
    ppermute x6, starting transfers between devices, shifted(): lax.ppermute(value, axis, [(source, source + steps) for source in range(i...  17.5 us
  transfers between devices with their start and end apart: 12, of which 12 were waited for; matrix products, arithmetic and copies ran while one was open for 0% of the time, Pallas kernels for 0%

commit v1 on v0

--- a/solution.py
+++ b/solution.py
@@ -32,7 +32,9 @@
 
     def precondition(residual):
         coarse = jnp.dot(basis_rows, residual, precision=lax.Precision.HIGHEST)
-        group_coarse = lax.all_gather(coarse, "sub", axis=0, tiled=True)
+        group_coarse = jnp.concatenate(
+            lax.all_to_all(jnp.stack([coarse] * lax.axis_size("sub")), "sub", 0, 0), axis=0
+        )
         solved = jnp.dot(inverse_rows, group_coarse, precision=lax.Precision.HIGHEST)
         spread_back = lax.dot_general(basis_rows, solved, contract, precision=lax.Precision.HIGHEST)
         return weight_col * residual + spread_back

time: 649 us -> 572 us (0.88)
  blocking collectives: 501 us -> 400 us
  starting transfers between devices: 21.9 us -> 35.2 us
  waiting for transfers between devices: 86.7 us -> 96 us
    all_gather x3 -> x0, blocking collectives: 128 us -> none  [precondition(): group_coarse = lax.all_gather(coarse, 'sub', axis=0, tiled=True)]
    all_to_all x0 -> x2, blocking collectives: none -> 30.9 us  [precondition(): lax.all_to_all(jnp.stack([coarse] * lax.axis_size('sub')), 'sub', 0, 0)]
    all_to_all x0 -> x1, starting transfers between devices: none -> 11.5 us  [precondition(): lax.all_to_all(jnp.stack([coarse] * lax.axis_size('sub')), 'sub', 0, 0)]
    all_to_all x0 -> x1, waiting for transfers between devices: none -> 9.01 us  [precondition(): lax.all_to_all(jnp.stack([coarse] * lax.axis_size('sub')), 'sub', 0, 0)]
  transfers between devices with their start and end apart: 12 -> 13, of which waited for: 12 -> 13; matrix products, arithmetic and copies ran while one was open for 0% -> 0% of each run, Pallas kernels for 0% -> 0%
where the time goes in v1:
time: 572 us; the launch traced here: 571 us
  blocking collectives  400 us (70%)
  waiting for transfers between devices  96 us (17%)
  starting transfers between devices  35.2 us (6%)
  matrix products  25.7 us (4%)
  local copies, waits for them, and re-layouts  7.61 us (1%)
    psum x3, blocking collectives, precond_inner(): return lax.psum(jnp.sum(residual * precond, axis=0), ('sub', 'grp'))  221 us
    psum x2, blocking collectives, local(): lax.psum(jnp.sum(direction * image, axis=0), ('sub', 'grp'))  148 us
    ppermute x6, waiting for transfers between devices, passed_along(): return lax.ppermute(block, axis, route)  52.7 us
    ppermute x6, waiting for transfers between devices, shifted(): lax.ppermute(value, axis, [(source, source + steps) for source in range(i...  34.3 us
    all_to_all x2, blocking collectives, precondition(): lax.all_to_all(jnp.stack([coarse] * lax.axis_size('sub')), 'sub', 0, 0)  30.9 us
    ppermute x6, starting transfers between devices, shifted(): lax.ppermute(value, axis, [(source, source + steps) for source in range(i...  19.1 us
    dot_general x3, matrix products, local(): product = jnp.dot(schur_block, stacked, preferred_element_type=jnp.float32)  18.8 us
    all_to_all x1, starting transfers between devices, precondition(): lax.all_to_all(jnp.stack([coarse] * lax.axis_size('sub')), 'sub', 0, 0)  11.5 us
  transfers between devices with their start and end apart: 13, of which 13 were waited for; matrix products, arithmetic and copies ran while one was open for 0% of the time, Pallas kernels for 0%

profile of v1, /device:TPU:2, one launch (start us, length us, event | category | flops | bytes accessed | tf_op | source)
XLA Modules:
  0.0 571.0 jit_solution(9917113931482594943)
XLA Ops:
  0.6 0.7 copy-done
  1.4 1.4 fusion.33
  2.8 0.7 stack.6
  3.5 11.5 %all-to-all-start = ((f32[32,8,128]{2,1,0:T(8,128)}), f32[32,8,128]{2,1,0:T(8,128)S(1)}, u32[]{:S(2)}, u32[]{:S(2)}) async-start(f32[32,8,128]{2,1,0:T(8,128)} %stack.6), calls=%async_computation | async-start | bytes 262144 | tf_op jit(solution)/shard_map/all_to_all | solution.py:36
  15.0 1.2 copy.8
  16.2 0.7 convert_element_type.34
  16.9 9.0 %all-to-all-done = f32[32,8,128]{2,1,0:T(8,128)S(1)} async-done(((f32[32,8,128]{2,1,0:T(8,128)}), f32[32,8,128]{2,1,0:T(8,128)S(1)}, u32[]{:S(2)}, u32[]{:S(2)}) %all-to-all-start) | async-done | bytes 131104 | tf_op jit(solution)/shard_map/all_to_all | solution.py:36
  25.9 1.1 fusion.40
  27.0 1.3 multiply_convert_fusion.2
  28.3 1.3 collective-permute-start
  29.6 6.7 %collective-permute-done = bf16[1024,128]{0,1:T(8,128)(2,1)S(1)} collective-permute-done((bf16[1024,128]{0,1:T(8,128)(2,1)S(1)}, bf16[1024,128]{0,1:T(8,128)(2,1)S(1)}, u32[]{:S(2)}, u32[]{:S(2)}) %collective-permute-start) | collective-permute-done | bytes 262176 | tf_op jit(solution)/shard_map/ppermute | solution.py:12
  36.4 2.4 collective-permute-start.1
  38.8 5.8 %collective-permute-done.1 = bf16[1024,128]{0,1:T(8,128)(2,1)S(1)} collective-permute-done((bf16[1024,128]{0,1:T(8,128)(2,1)S(1)}, bf16[1024,128]{0,1:T(8,128)(2,1)S(1)}, u32[]{:S(2)}, u32[]{:S(2)}) %collective-permute-start.1) | collective-permute-done | bytes 262176 | tf_op jit(solution)/shard_map/ppermute | solution.py:18
  44.6 6.3 %fusion.6 = f32[2048,128]{0,1:T(8,128)S(1)} fusion(bf16[1,1,2048,2048]{3,2,1,0:T(8,128)(2,1)} %param.7, bf16[1024,128]{0,1:T(8,128)(2,1)S(1)} %broadcast_select_fusion.2, bf16[1024,128]{0,1:T(8,128)(2,1)S(1)} %get-tuple-element.14), kind=kOutput, calls=%fused_computation.6 | convolution fusion | flops 1074790400 | bytes 9961472 | tf_op jit(solution)/shard_map/dot_general | solution.py:56
  51.1 12.2 %collective-permute-done.2 = bf16[1024,128]{0,1:T(8,128)(2,1)S(1)} collective-permute-done((bf16[1024,128]{0,1:T(8,128)(2,1)S(1)}, bf16[1024,128]{0,1:T(8,128)(2,1)S(1)}, u32[]{:S(2)}, u32[]{:S(2)}) %collective-permute-start.2) | collective-permute-done | bytes 262176 | tf_op jit(solution)/shard_map/ppermute | solution.py:12
  63.2 3.4 collective-permute-start.3
  66.7 4.8 collective-permute-done.3
  71.8 74.5 %all-reduce = (f32[128]{0:T(128)S(1)}, f32[128]{0:T(128)S(1)}) all-reduce(f32[128]{0:T(128)S(1)} %get-tuple-element.5, f32[128]{0:T(128)S(1)} %get-tuple-element.4), channel_id=1, replica_groups=mesh['sub'=32,'grp'=8] {'sub','grp'}, use_global_device_ids=true, to_apply=%region_1.0 | all-reduce | flops 256 | bytes 2048 | tf_op jit(solution)/shard_map/psum | solution.py:43
  146.5 0.5 convolution_bitcast_fusion.4
  147.0 16.0 %all_to_all.15 = f32[32,8,128]{2,1,0:T(8,128)S(1)} all-to-all(f32[32,8,128]{2,1,0:T(8,128)S(1)} %stack.7), channel_id=1, replica_groups=mesh['sub'=32,'grp'=8] {'sub'}, dimensions={0} | all-to-all | bytes 262144 | tf_op jit(solution)/shard_map/all_to_all | solution.py:36
  163.5 0.7 multiply_reduce_fusion.3
  164.1 73.1 %psum.44 = f32[128]{0:T(128)S(1)} all-reduce(f32[128]{0:T(128)S(1)} %get-tuple-element.16), channel_id=1, replica_groups=mesh['sub'=32,'grp'=8] {'sub','grp'}, use_global_device_ids=true, to_apply=%region_5.6 | all-reduce | flops 128 | bytes 1024 | tf_op jit(solution)/shard_map/psum | solution.py:43
  237.4 1.6 collective-permute-start.4
  239.0 4.0 collective-permute-done.4
  243.0 3.9 collective-permute-start.5
  246.9 6.3 %collective-permute-done.5 = bf16[1024,128]{0,1:T(8,128)(2,1)S(1)} collective-permute-done((bf16[1024,128]{0,1:T(8,128)(2,1)S(1)}, bf16[1024,128]{0,1:T(8,128)(2,1)S(1)}, u32[]{:S(2)}, u32[]{:S(2)}) %collective-permute-start.5) | collective-permute-done | bytes 262176 | tf_op jit(solution)/shard_map/ppermute | solution.py:18
  253.2 6.3 %fusion.9 = f32[2048,128]{0,1:T(8,128)S(1)} fusion(bf16[1,1,2048,2048]{3,2,1,0:T(8,128)(2,1)} %param.7, bf16[1024,128]{0,1:T(8,128)(2,1)S(1)} %broadcast_select_fusion.1, bf16[1024,128]{0,1:T(8,128)(2,1)S(1)} %get-tuple-element.10), kind=kOutput, calls=%fused_computation.7 | convolution fusion | flops 1074790400 | bytes 9961472 | tf_op jit(solution)/shard_map/dot_general | solution.py:56
  259.6 12.8 %collective-permute-done.6 = bf16[1024,128]{0,1:T(8,128)(2,1)S(1)} collective-permute-done((bf16[1024,128]{0,1:T(8,128)(2,1)S(1)}, bf16[1024,128]{0,1:T(8,128)(2,1)S(1)}, u32[]{:S(2)}, u32[]{:S(2)}) %collective-permute-start.6) | collective-permute-done | bytes 262176 | tf_op jit(solution)/shard_map/ppermute | solution.py:12
  272.4 2.8 collective-permute-start.7
  275.2 5.5 collective-permute-done.7
  280.9 74.3 %psum.45 = f32[128]{0:T(128)S(1)} all-reduce(f32[128]{0:T(128)S(1)} %multiply_reduce_fusion.2), channel_id=1, replica_groups=mesh['sub'=32,'grp'=8] {'sub','grp'}, use_global_device_ids=true, to_apply=%region_7.8 | all-reduce | flops 128 | bytes 1024 | tf_op jit(solution)/shard_map/psum | solution.py:65
  355.3 1.1 multiply_subtract_fusion
  356.9 14.9 %all_to_all.16 = f32[32,8,128]{2,1,0:T(8,128)S(1)} all-to-all(f32[32,8,128]{2,1,0:T(8,128)S(1)} %stack.8), channel_id=1, replica_groups=mesh['sub'=32,'grp'=8] {'sub'}, dimensions={0} | all-to-all | bytes 262144 | tf_op jit(solution)/shard_map/all_to_all | solution.py:36
  372.2 0.7 multiply_reduce_fusion.1
  372.9 73.4 %psum.46 = f32[128]{0:T(128)S(1)} all-reduce(f32[128]{0:T(128)S(1)} %get-tuple-element.18), channel_id=1, replica_groups=mesh['sub'=32,'grp'=8] {'sub','grp'}, use_global_device_ids=true, to_apply=%region_9.10 | all-reduce | flops 128 | bytes 1024 | tf_op jit(solution)/shard_map/psum | solution.py:43
  446.5 1.5 collective-permute-start.8
  447.9 4.0 collective-permute-done.8
  451.9 3.8 collective-permute-start.9
  455.8 6.5 %collective-permute-done.9 = bf16[1024,128]{0,1:T(8,128)(2,1)S(1)} collective-permute-done((bf16[1024,128]{0,1:T(8,128)(2,1)S(1)}, bf16[1024,128]{0,1:T(8,128)(2,1)S(1)}, u32[]{:S(2)}, u32[]{:S(2)}) %collective-permute-start.9) | collective-permute-done | bytes 262176 | tf_op jit(solution)/shard_map/ppermute | solution.py:18
  462.3 6.3 %fusion.12 = f32[2048,128]{0,1:T(8,128)S(1)} fusion(bf16[1,1,2048,2048]{3,2,1,0:T(8,128)(2,1)} %param.7, bf16[1024,128]{0,1:T(8,128)(2,1)S(1)} %broadcast_select_fusion, bf16[1024,128]{0,1:T(8,128)(2,1)S(1)} %get-tuple-element.8), kind=kOutput, calls=%fused_computation.8 | convolution fusion | flops 1074790400 | bytes 9961472 | tf_op jit(solution)/shard_map/dot_general | solution.py:56
  468.7 12.8 %collective-permute-done.10 = bf16[1024,128]{0,1:T(8,128)(2,1)S(1)} collective-permute-done((bf16[1024,128]{0,1:T(8,128)(2,1)S(1)}, bf16[1024,128]{0,1:T(8,128)(2,1)S(1)}, u32[]{:S(2)}, u32[]{:S(2)}) %collective-permute-start.10) | collective-permute-done | bytes 262176 | tf_op jit(solution)/shard_map/ppermute | solution.py:12
  481.5 2.8 collective-permute-start.11
  484.4 5.5 collective-permute-done.11
  489.8 0.7 copy-done.2
  490.7 74.0 %psum.47 = f32[128]{0:T(128)S(1)} all-reduce(f32[128]{0:T(128)S(1)} %multiply_reduce_fusion), channel_id=1, replica_groups=mesh['sub'=32,'grp'=8] {'sub','grp'}, use_global_device_ids=true, to_apply=%region_11.12 | all-reduce | flops 128 | bytes 1024 | tf_op jit(solution)/shard_map/psum | solution.py:65
  564.8 2.2 subtract_bitcast_fusion
  567.0 2.0 copy.10
  569.0 2.0 copy.9
  (34 shorter events, 3.0 us)
Async XLA Ops:
  0.6 0.8 copy-start
  3.5 22.4 %all-to-all-start = ((f32[32,8,128]{2,1,0:T(8,128)}), f32[32,8,128]{2,1,0:T(8,128)S(1)}, u32[]{:S(2)}, u32[]{:S(2)}) async-start(f32[32,8,128]{2,1,0:T(8,128)} %stack.6), calls=%async_computation | async-start | bytes 262144 | tf_op jit(solution)/shard_map/all_to_all | solution.py:36
  28.3 8.1 %collective-permute-start = (bf16[1024,128]{0,1:T(8,128)(2,1)S(1)}, bf16[1024,128]{0,1:T(8,128)(2,1)S(1)}, u32[]{:S(2)}, u32[]{:S(2)}) collective-permute-start(bf16[1024,128]{0,1:T(8,128)(2,1)S(1)} %get-tuple-element.14), channel_id=1, source_target_pairs={{8,0},{16,8},{24,16},{32,24},{40,32},{48,40},{56,48},{64,56},{72,6... | collective-permute-start | bytes 786440 | tf_op jit(solution)/shard_map/ppermute | solution.py:12
  36.4 8.3 %collective-permute-start.1 = (bf16[1024,128]{0,1:T(8,128)(2,1)S(1)}, bf16[1024,128]{0,1:T(8,128)(2,1)S(1)}, u32[]{:S(2)}, u32[]{:S(2)}) collective-permute-start(bf16[1024,128]{0,1:T(8,128)(2,1)S(1)} %collective-permute-done), channel_id=1, source_target_pairs={{1,0},{2,1},{3,2},{4,3},{5,4},{6,5},{7,6},{9,8},{10,9},{11,10},{12... | collective-permute-start | bytes 786440 | tf_op jit(solution)/shard_map/ppermute | solution.py:18
  38.8 124.3 %copy-start.3 = (f32[1,8,256]{2,1,0:T(8,128)S(1)}, f32[1,8,256]{2,1,0:T(8,128)}, u32[]{:S(2)}) copy-start(f32[1,8,256]{2,1,0:T(8,128)} %param.11) | copy-start | bytes 24580
  44.6 118.8 %copy-start.4 = (f32[1,1,1024]{2,1,0:T(1,128)S(1)}, f32[1,1,1024]{2,1,0:T(1,128)}, u32[]{:S(2)}) copy-start(f32[1,1,1024]{2,1,0:T(1,128)} %param.9) | copy-start | bytes 12292
  51.0 12.3 %collective-permute-start.2 = (bf16[1024,128]{0,1:T(8,128)(2,1)S(1)}, bf16[1024,128]{0,1:T(8,128)(2,1)S(1)}, u32[]{:S(2)}, u32[]{:S(2)}) collective-permute-start(bf16[1024,128]{0,1:T(8,128)(2,1)S(1)} %slice.65), channel_id=1, source_target_pairs={{248,0},{0,8},{8,16},{16,24},{24,32},{32,40},{40,48},{48,56},{56,6... | collective-permute-start | bytes 786440 | tf_op jit(solution)/shard_map/ppermute | solution.py:12
  63.2 8.3 %collective-permute-start.3 = (bf16[1024,128]{0,1:T(8,128)(2,1)S(1)}, bf16[1024,128]{0,1:T(8,128)(2,1)S(1)}, u32[]{:S(2)}, u32[]{:S(2)}) collective-permute-start(bf16[1024,128]{0,1:T(8,128)(2,1)S(1)} %collective-permute-done.2), channel_id=1, source_target_pairs={{0,1},{1,2},{2,3},{3,4},{4,5},{5,6},{6,7},{8,9},{9,10},{10,11},{11... | collective-permute-start | bytes 786440 | tf_op jit(solution)/shard_map/ppermute | solution.py:18
  237.4 5.6 collective-permute-start.4
  243.0 10.2 %collective-permute-start.5 = (bf16[1024,128]{0,1:T(8,128)(2,1)S(1)}, bf16[1024,128]{0,1:T(8,128)(2,1)S(1)}, u32[]{:S(2)}, u32[]{:S(2)}) collective-permute-start(bf16[1024,128]{0,1:T(8,128)(2,1)S(1)} %collective-permute-done.4), channel_id=1, source_target_pairs={{1,0},{2,1},{3,2},{4,3},{5,4},{6,5},{7,6},{9,8},{10,9},{11,10},{12... | collective-permute-start | bytes 786440 | tf_op jit(solution)/shard_map/ppermute | solution.py:18
  259.5 12.9 %collective-permute-start.6 = (bf16[1024,128]{0,1:T(8,128)(2,1)S(1)}, bf16[1024,128]{0,1:T(8,128)(2,1)S(1)}, u32[]{:S(2)}, u32[]{:S(2)}) collective-permute-start(bf16[1024,128]{0,1:T(8,128)(2,1)S(1)} %slice.64), channel_id=1, source_target_pairs={{248,0},{0,8},{8,16},{16,24},{24,32},{32,40},{40,48},{48,56},{56,6... | collective-permute-start | bytes 786440 | tf_op jit(solution)/shard_map/ppermute | solution.py:12
  272.4 8.3 %collective-permute-start.7 = (bf16[1024,128]{0,1:T(8,128)(2,1)S(1)}, bf16[1024,128]{0,1:T(8,128)(2,1)S(1)}, u32[]{:S(2)}, u32[]{:S(2)}) collective-permute-start(bf16[1024,128]{0,1:T(8,128)(2,1)S(1)} %collective-permute-done.6), channel_id=1, source_target_pairs={{0,1},{1,2},{2,3},{3,4},{4,5},{5,6},{6,7},{8,9},{9,10},{10,11},{11... | collective-permute-start | bytes 786440 | tf_op jit(solution)/shard_map/ppermute | solution.py:18
  280.7 74.6 %copy-start.1 = (bf16[1024,128]{0,1:T(8,128)(2,1)}, bf16[1024,128]{0,1:T(8,128)(2,1)S(1)}, u32[]{:S(2)}) copy-start(bf16[1024,128]{0,1:T(8,128)(2,1)S(1)} %collective-permute-done.7) | copy-start | bytes 786436
  446.5 5.5 collective-permute-start.8
  451.9 10.3 %collective-permute-start.9 = (bf16[1024,128]{0,1:T(8,128)(2,1)S(1)}, bf16[1024,128]{0,1:T(8,128)(2,1)S(1)}, u32[]{:S(2)}, u32[]{:S(2)}) collective-permute-start(bf16[1024,128]{0,1:T(8,128)(2,1)S(1)} %collective-permute-done.8), channel_id=1, source_target_pairs={{1,0},{2,1},{3,2},{4,3},{5,4},{6,5},{7,6},{9,8},{10,9},{11,10},{12... | collective-permute-start | bytes 786440 | tf_op jit(solution)/shard_map/ppermute | solution.py:18
  468.6 12.9 %collective-permute-start.10 = (bf16[1024,128]{0,1:T(8,128)(2,1)S(1)}, bf16[1024,128]{0,1:T(8,128)(2,1)S(1)}, u32[]{:S(2)}, u32[]{:S(2)}) collective-permute-start(bf16[1024,128]{0,1:T(8,128)(2,1)S(1)} %slice.63), channel_id=1, source_target_pairs={{248,0},{0,8},{8,16},{16,24},{24,32},{32,40},{40,48},{48,56},{56,6... | collective-permute-start | bytes 786440 | tf_op jit(solution)/shard_map/ppermute | solution.py:12
  481.5 8.3 %collective-permute-start.11 = (bf16[1024,128]{0,1:T(8,128)(2,1)S(1)}, bf16[1024,128]{0,1:T(8,128)(2,1)S(1)}, u32[]{:S(2)}, u32[]{:S(2)}) collective-permute-start(bf16[1024,128]{0,1:T(8,128)(2,1)S(1)} %collective-permute-done.10), channel_id=1, source_target_pairs={{0,1},{1,2},{2,3},{3,4},{4,5},{5,6},{6,7},{8,9},{9,10},{10,11},{11... | collective-permute-start | bytes 786440 | tf_op jit(solution)/shard_map/ppermute | solution.py:18
  489.8 0.7 copy-start.2
